TPU v7x, 128 devices: a whole 4x4x4 slice. The times are simulated.
128 devices in a mesh: dev: 128 (over x, y, z, core).
Axes of the slice: x: 4, y: 4, z: 4, core: 2. Of those that a mesh axis runs over, the one named last changes fastest.
Arguments:
- params: float32 [9, 131072], P(None, 'dev')
- moment: float32 [9, 131072], P(None, 'dev'), may hold values from -3 to 3
- second: float32 [9, 131072], P(None, 'dev'), may hold values from 0.05 to 1
- fetch_ids: int32 [128, 128, 8], P('dev'), may hold values from 0 to 1023
- seg_ids: int32 [512, 256], P('dev'), may hold values from 0 to 1023
- seg_count: int32 [512], P('dev'), may hold values from 1 to 256, 98304 in all
- seg_perm: int32 [512], replicated, may hold values from 0 to 511, as said below
- target: float32 [128, 3, 256], P('dev'), may hold values from 0 to 1
Outputs:
- image: float32 [128, 3, 256], P('dev')
- new_params: float32 [9, 131072], P(None, 'dev')
- new_moment: float32 [9, 131072], P(None, 'dev')
- new_second: float32 [9, 131072], P(None, 'dev')
Inputs may be any that keep to these rules, and one draw needn't show every extreme that they name: `seg_count`: segments that exceed their count hold unused slots; some segment is full. `seg_perm`: each number appears once.
All inputs are finite; a program needn't handle non-finite values. No bound on the sum of `seg_count` on one device may be relied on, other than what follows from the above.
Results may differ from a plain program's by a relative error of at most 0.0003.
Values sent between devices are 32-bit elements; how exact they have to be, the bound alone decides.
A program may use at most 192 MiB of HBM per device.

v0:
```python
import jax
import jax.numpy as jnp
from jax import lax
from jax.sharding import PartitionSpec as P

TILES_X = 8
KSEG = 4


def segment(par, count, tile):
    span = par.shape[1]
    pidx = jnp.arange(256, dtype=jnp.int32)
    fine_x = ((pidx % 16).astype(jnp.float32) + 0.5) / 16.0
    fine_y = ((pidx // 16).astype(jnp.float32) + 0.5) / 16.0
    pos_x = (tile % TILES_X).astype(jnp.float32) + fine_x
    pos_y = (tile // TILES_X).astype(jnp.float32) + fine_y
    steps = jnp.arange(span, dtype=jnp.int32)
    live = (steps < count).astype(jnp.float32)
    delta_x = pos_x[None, :] - par[0][:, None]
    delta_y = pos_y[None, :] - par[1][:, None]
    scale_a = jnp.exp(par[2])
    scale_c = jnp.exp(par[3])
    cross = 0.8 * jnp.tanh(par[4]) * scale_a * scale_c
    power = -0.5 * (
        (scale_a * scale_a)[:, None] * delta_x * delta_x
        + 2.0 * cross[:, None] * delta_x * delta_y
        + (scale_c * scale_c)[:, None] * delta_y * delta_y
    )
    alpha = (0.95 * jax.nn.sigmoid(par[5]) * live)[:, None] * jnp.exp(power)
    logt = jnp.log1p(-alpha)
    lower = (steps[:, None] > steps[None, :]).astype(jnp.float32)
    earlier = jnp.dot(lower, logt, precision=lax.Precision.HIGHEST)
    weight = jnp.exp(earlier) * alpha
    colour = jnp.dot(par[6:9], weight, precision=lax.Precision.HIGHEST)
    return (colour, jnp.sum(logt, axis=0))


def per_device(params, moment, second, fetch_ids, seg_ids, seg_count, seg_perm, target):
    ndev = lax.axis_size("dev")
    me = lax.axis_index("dev")
    nparam, owned = params.shape
    segs, span = seg_ids.shape
    tiles_dev = target.shape[0]
    pixels = target.shape[2]
    wanted = fetch_ids[0]
    cap = wanted.shape[1]
    received = lax.all_to_all(wanted, "dev", split_axis=0, concat_axis=0, tiled=True)
    buckets = jnp.take(params, received, axis=1)
    arrived = lax.all_to_all(buckets, "dev", split_axis=1, concat_axis=1, tiled=True)
    buffer = arrived.reshape(nparam, ndev * cap)
    first = me * segs
    own_perm = lax.dynamic_slice_in_dim(seg_perm, first, segs, 0)
    own_tile = own_perm // KSEG
    own_rank = own_perm % KSEG
    gathered_par = jnp.moveaxis(jnp.take(buffer, seg_ids, axis=1), 1, 0)

    def partials(values):
        return jax.vmap(segment)(values, seg_count, own_tile)

    (colours, logs), back = jax.vjp(partials, gathered_par)
    all_colours, all_logs, all_target = (
        lax.all_gather(colours, "dev", axis=0, tiled=True),
        lax.all_gather(logs, "dev", axis=0, tiled=True),
        lax.all_gather(target, "dev", axis=0, tiled=True),
    )
    total = all_logs.shape[0]
    ntiles = all_target.shape[0]
    tile_all = seg_perm // KSEG
    rank_all = seg_perm % KSEG
    same = tile_all[:, None] == tile_all[None, :]
    before = (same & (rank_all[None, :] < rank_all[:, None])).astype(jnp.float32)
    prefix = jnp.exp(jnp.dot(before, all_logs, precision=lax.Precision.HIGHEST))
    contrib = (prefix[:, None, :] * all_colours).reshape(total, 3 * pixels)
    onehot = (jnp.arange(ntiles, dtype=jnp.int32)[:, None] == tile_all[None, :]).astype(jnp.float32)
    image = jnp.dot(onehot, contrib, precision=lax.Precision.HIGHEST)
    misfit = image - all_target.reshape(ntiles, 3 * pixels)
    later = (
        (own_tile[:, None] == tile_all[None, :]) & (rank_all[None, :] > own_rank[:, None])
    ).astype(jnp.float32)
    behind = jnp.dot(later, contrib, precision=lax.Precision.HIGHEST).reshape(segs, 3, pixels)
    picker = (own_tile[:, None] == jnp.arange(ntiles, dtype=jnp.int32)[None, :]).astype(jnp.float32)
    error = jnp.dot(picker, misfit, precision=lax.Precision.HIGHEST).reshape(segs, 3, pixels)
    own_prefix = lax.dynamic_slice_in_dim(prefix, first, segs, 0)
    d_colour = own_prefix[:, None, :] * error
    d_log = jnp.sum(error * behind, axis=1)
    (d_par,) = back((d_colour, d_log))
    slot_grad = (
        jnp.zeros((nparam, ndev * cap), jnp.float32)
        .at[:, seg_ids.reshape(-1)]
        .add(jnp.moveaxis(d_par, 1, 0).reshape(nparam, segs * span))
    )
    returned = lax.all_to_all(
        slot_grad.reshape(nparam, ndev, cap), "dev", split_axis=1, concat_axis=1, tiled=True
    )
    grad = (
        jnp.zeros((nparam, owned), jnp.float32)
        .at[:, received.reshape(-1)]
        .add(returned.reshape(nparam, ndev * cap))
    )
    new_moment = 0.9 * moment + 0.1 * grad
    new_second = 0.99 * second + 0.01 * grad * grad
    new_params = params - 0.05 * new_moment / (jnp.sqrt(new_second) + 1e-08)
    my_image = lax.dynamic_slice_in_dim(image, me * tiles_dev, tiles_dev, 0).reshape(
        tiles_dev, 3, pixels
    )
    return (my_image, new_params, new_moment, new_second)


def solution(mesh):
    placed = (
        P(None, "dev"),
        P(None, "dev"),
        P(None, "dev"),
        P("dev", None, None),
        P("dev", None),
        P("dev"),
        P(),
        P("dev", None, None),
    )
    return jax.shard_map(
        per_device,
        mesh=mesh,
        in_specs=placed,
        out_specs=(P("dev", None, None), P(None, "dev"), P(None, "dev"), P(None, "dev")),
        check_vma=False,
    )
```

profile of v0, /device:TPU:1, one launch (start us, length us, event | category | flops | bytes accessed | tf_op | source)
XLA Modules:
  0.0 180.8 jit_solution(5734400977405865448)
XLA Ops:
  7.2 1.4 copy.73
  8.6 11.5 %all-to-all-start = ((s32[128,1,8]{2,1,0:T(1,128)}), s32[128,1,8]{2,1,0:T(1,128)S(1)}, u32[]{:S(2)}, u32[]{:S(2)}) async-start(s32[128,1,8]{2,1,0:T(1,128)} %bitcast), calls=%async_computation | async-start | bytes 131072 | tf_op jit(solution)/shard_map/all_to_all | solution.py:47
  20.1 0.7 fusion.92
  20.8 0.7 compare_and_fusion.1
  21.5 0.8 and_select_fusion
  22.3 0.8 fusion.102
  23.0 0.1 broadcast_add_fusion.1
  23.1 1.1 copy.74
  24.2 5.2 %all-to-all-done = s32[128,1,8]{2,1,0:T(1,128)S(1)} async-done(((s32[128,1,8]{2,1,0:T(1,128)}), s32[128,1,8]{2,1,0:T(1,128)S(1)}, u32[]{:S(2)}, u32[]{:S(2)}) %all-to-all-start) | async-done | bytes 4128 | tf_op jit(solution)/shard_map/all_to_all | solution.py:47
  29.4 0.1 reshape.400
  29.5 2.8 %gather_fusion = f32[1024,9]{1,0:T(8,128)S(1)} fusion(f32[9,1024]{0,1:T(8,128)S(1)} %copy.74, s32[1024]{0:T(1024)S(1)} %broadcast_clamp_fusion.1), kind=kCustom, calls=%fused_computation | custom fusion | bytes 77824 | tf_op jit(solution)/shard_map/jit(_take)/gather | solution.py:48
  32.3 0.0 copy-start.6
  32.4 1.0 fusion.43
  33.4 4.8 %all-to-all-start.1 = ((f32[9,128,8]{0,2,1:T(8,128)}), f32[9,128,8]{0,2,1:T(8,128)S(1)}, u32[]{:S(2)}, u32[]{:S(2)}) async-start(f32[9,128,8]{0,2,1:T(8,128)} %fusion.43), calls=%async_computation.1 | async-start | bytes 1048576 | tf_op jit(solution)/shard_map/all_to_all | solution.py:49
  38.1 0.0 all-gather.3.cloned.1.call-start
  38.2 13.5 %all-to-all-done.1 = f32[9,128,8]{0,2,1:T(8,128)S(1)} async-done(((f32[9,128,8]{0,2,1:T(8,128)}), f32[9,128,8]{0,2,1:T(8,128)S(1)}, u32[]{:S(2)}, u32[]{:S(2)}) %all-to-all-start.1) | async-done | bytes 36896 | tf_op jit(solution)/shard_map/all_to_all | solution.py:49
  51.7 2.8 %gather_fusion.1 = f32[1024,9]{1,0:T(8,128)S(1)} fusion(f32[9,1024]{0,1:T(8,128)S(1)} %bitcast.116, s32[1024]{0:T(1024)S(1)} %broadcast_clamp_fusion), kind=kCustom, calls=%fused_computation.1 | custom fusion | bytes 77824 | tf_op jit(solution)/shard_map/jit(_take)/gather | solution.py:55
  54.5 0.2 copy.76
  54.8 0.0 copy-done.6
  54.8 0.1 bitcast_select_fusion.1
  54.9 1.5 convolution_exponential_fusion
  56.3 0.0 copy-start.7
  56.3 0.0 copy-start.3
  56.4 0.0 copy-start.5
  56.4 2.1 %fusion.60 = f32[4,3,256]{2,1,0:T(4,128)} fusion(f32[256,4,256]{0,2,1:T(8,128)S(1)} %convolution_exponential_fusion, f32[4,256]{1,0:T(4,128)S(1)} %get-tuple-element.48, f32[4,256]{1,0:T(4,128)S(1)} %get-tuple-element.51, f32[4,256]{1,0:T(4,128)S(1)} %get-tuple-element.56, f32[4,256]{1,0:T(4,128)S(1)} %get-tuple-element.44, ...), kind=kOutput, calls=%fused_computation.86 | convolution fusion | flops 12845056 | bytes 1110016 | tf_op jit(solution)/shard_map/jvp(vmap())/dot_general | solution.py:34
  58.5 0.0 copy-done.7
  58.5 0.0 all-gather.3.cloned.1.call-update
  58.5 0.0 copy-done.3
  58.5 33.7 %all_gather.11 = f32[128,3,256]{2,1,0:T(4,128)S(1)} all-gather(f32[1,3,256]{2,1,0:T(4,128)S(1)} %copy.80), channel_id=1, replica_groups=mesh['dev'=128] {'dev'}, dimensions={0}, use_global_device_ids=true | all-gather | bytes 396288 | tf_op jit(solution)/shard_map/all_gather | solution.py:64
  92.3 0.2 copy.81
  92.5 0.2 copy.82
  92.7 0.0 copy-done.4
  92.7 0.5 broadcast.499
  93.2 0.8 reduce.3
  94.0 0.1 reshape.387
  94.1 1.0 log-plus-one_reduce_fusion
  95.2 35.5 %all-gather = f32[128,4,256]{2,1,0:T(4,128)S(1)} all-gather(f32[1,4,256]{2,1,0:T(4,128)S(1)} %bitcast.127), channel_id=1, replica_groups=mesh['dev'=128] {'dev'}, dimensions={0}, use_global_device_ids=true | all-gather | bytes 528384 | tf_op jit(solution)/shard_map/all_gather | solution.py:63
  130.7 0.2 reshape.434
  130.9 0.7 convolution_exponential_fusion.1
  131.6 0.2 copy.77
  131.8 0.0 all-gather.3.cloned.1.call-done
  131.9 1.8 %copy.79 = f32[512,3,256]{0,2,1:T(8,128)S(1)} copy(f32[512,3,256]{2,1,0:T(4,128)} %all-gather.3.cloned.1.call-done) | data formatting | bytes 3145728 | tf_op jit(solution)/shard_map/all_gather | solution.py:62
  133.7 0.2 broadcast_multiply_fusion
  133.9 1.0 fusion.66
  134.9 0.3 fusion.61
  135.2 1.1 fusion.72
  136.3 0.0 copy-done.8
  136.3 1.2 fusion.59
  137.5 0.8 fusion.12
  138.3 3.0 %fusion.33 = (f32[4,256]{1,0:T(4,128)S(1)}, f32[4,256]{1,0:T(4,128)S(1)}, f32[4,256]{1,0:T(4,128)S(1)}, f32[4,256]{1,0:T(4,128)S(1)}, f32[4,256]{1,0:T(4,128)S(1)}, /*index=5*/f32[4,256]{1,0:T(4,128)S(1)}) fusion(f32[4,256]{1,0:T(4,128)S(1)} %get-tuple-element.51, f32[4,256]{1,0:T(4,128)S(1)} %get-tuple-element.56, f32[4,256]{1,0:T(4,128)S(1)} %get-tuple-element.48, ...), kind=kOutput, calls=%fused_computation.52 | convolution fusion | flops 820570112 | bytes 2183168 | tf_op jit(solution)/shard_map/transpose(jvp(vmap()))/dot_general | solution.py:32
  141.4 0.1 fusion.81
  141.5 0.1 add_bitcast_fusion
  141.7 0.2 copy.87
  141.9 0.0 copy-start
  141.9 0.0 copy-start.1
  141.9 0.0 copy-start.2
  141.9 6.8 %scatter_custom_fusion = f32[9,1024]{0,1:T(8,128)} fusion(s32[1024]{0:T(1024)S(1)} %bitcast.130, f32[1024,9]{1,0:T(8,128)S(1)} %copy.87, f32[]{:T(128)} %constant.149.clone.1), kind=kCustom, calls=%fused_computation.90 | custom fusion | flops 9216 | bytes 36868 | tf_op jit(solution)/shard_map/scatter-add | solution.py:90
  148.7 4.6 %all-to-all-start.2 = ((f32[9,128,8]{0,2,1:T(8,128)}), f32[9,128,8]{0,2,1:T(8,128)S(1)}, u32[]{:S(2)}, u32[]{:S(2)}) async-start(f32[9,128,8]{0,2,1:T(8,128)} %bitcast.30), calls=%async_computation.2 | async-start | bytes 1048576 | tf_op jit(solution)/shard_map/all_to_all | solution.py:92
  153.4 0.6 constant_dynamic-slice_fusion.1
  154.0 13.0 %all-to-all-done.2 = f32[9,128,8]{0,2,1:T(8,128)S(1)} async-done(((f32[9,128,8]{0,2,1:T(8,128)}), f32[9,128,8]{0,2,1:T(8,128)S(1)}, u32[]{:S(2)}, u32[]{:S(2)}) %all-to-all-start.2) | async-done | bytes 36896 | tf_op jit(solution)/shard_map/all_to_all | solution.py:92
  166.9 6.2 %scatter_custom_fusion.1 = f32[9,1024]{0,1:T(8,128)S(1)} fusion(s32[1024]{0:T(1024)S(1)} %bitcast.129, f32[9,128,8]{0,2,1:T(8,128)S(1)} %all-to-all-done.2, f32[]{:T(128)} %constant.149.clone.1), kind=kCustom, calls=%fused_computation.67 | custom fusion | flops 9216 | bytes 561156 | tf_op jit(solution)/shard_map/scatter-add | solution.py:98
  173.1 0.2 copy.88
  173.3 0.0 copy-done.2
  173.3 0.7 divide_subtract_fusion
  (34 shorter events, 0.3 us)
Async XLA Ops:
  8.6 20.8 %all-to-all-start = ((s32[128,1,8]{2,1,0:T(1,128)}), s32[128,1,8]{2,1,0:T(1,128)S(1)}, u32[]{:S(2)}, u32[]{:S(2)}) async-start(s32[128,1,8]{2,1,0:T(1,128)} %bitcast), calls=%async_computation | async-start | bytes 131072 | tf_op jit(solution)/shard_map/all_to_all | solution.py:47
  32.3 22.4 %copy-start.6 = (s32[4]{0:T(128)S(1)}, s32[4]{0:T(128)}, u32[]{:S(2)}) copy-start(s32[4]{0:T(128)} %param.13) | copy-start | bytes 52
  33.4 18.3 %all-to-all-start.1 = ((f32[9,128,8]{0,2,1:T(8,128)}), f32[9,128,8]{0,2,1:T(8,128)S(1)}, u32[]{:S(2)}, u32[]{:S(2)}) async-start(f32[9,128,8]{0,2,1:T(8,128)} %fusion.43), calls=%async_computation.1 | async-start | bytes 1048576 | tf_op jit(solution)/shard_map/all_to_all | solution.py:49
  38.1 93.7 %all-gather.3.cloned.1.call-start = ((), (), s32[]{:S(2)}) async-start(), calls=%async_computation.3 | async-start | bytes 2113536 | tf_op jit(solution)/shard_map/all_gather | solution.py:62
  56.3 2.1 %copy-start.7 = (f32[256,4,256]{0,2,1:T(8,128)}, f32[256,4,256]{0,2,1:T(8,128)S(1)}, u32[]{:S(2)}) copy-start(f32[256,4,256]{0,2,1:T(8,128)S(1)} %convolution_exponential_fusion) | copy-start | bytes 3145732
  56.3 2.2 %copy-start.3 = (s32[4,256]{1,0:T(4,128)S(1)}, s32[4,256]{1,0:T(4,128)}, u32[]{:S(2)}) copy-start(s32[4,256]{1,0:T(4,128)} %param.12) | copy-start | bytes 12292
  56.4 2.2 %copy-start.5 = (f32[1,3,256]{2,0,1:T(1,128)S(1)}, f32[1,3,256]{2,0,1:T(1,128)}, u32[]{:S(2)}) copy-start(f32[1,3,256]{2,0,1:T(1,128)} %param.15) | copy-start | bytes 9220
  58.5 34.2 %copy-start.4 = (s32[512]{0:T(512)S(1)}, s32[512]{0:T(512)}, u32[]{:S(2)}) copy-start(s32[512]{0:T(512)} %param.14) | copy-start | bytes 6148
  133.9 2.4 %copy-start.8 = (f32[256,4,256]{0,2,1:T(8,128)S(1)}, f32[256,4,256]{0,2,1:T(8,128)}, u32[]{:S(2)}) copy-start(f32[256,4,256]{0,2,1:T(8,128)} %copy-done.7) | copy-start | bytes 3145732
  141.9 31.4 %copy-start = (f32[9,1024]{1,0:T(8,128)S(1)}, f32[9,1024]{1,0:T(8,128)}, u32[]{:S(2)}) copy-start(f32[9,1024]{1,0:T(8,128)} %param.8) | copy-start | bytes 110596
  141.9 31.4 %copy-start.1 = (f32[9,1024]{1,0:T(8,128)S(1)}, f32[9,1024]{1,0:T(8,128)}, u32[]{:S(2)}) copy-start(f32[9,1024]{1,0:T(8,128)} %param.9) | copy-start | bytes 110596
  141.9 31.4 %copy-start.2 = (f32[9,1024]{1,0:T(8,128)S(1)}, f32[9,1024]{1,0:T(8,128)}, u32[]{:S(2)}) copy-start(f32[9,1024]{1,0:T(8,128)} %param.10) | copy-start | bytes 110596
  148.7 18.2 %all-to-all-start.2 = ((f32[9,128,8]{0,2,1:T(8,128)}), f32[9,128,8]{0,2,1:T(8,128)S(1)}, u32[]{:S(2)}, u32[]{:S(2)}) async-start(f32[9,128,8]{0,2,1:T(8,128)} %bitcast.30), calls=%async_computation.2 | async-start | bytes 1048576 | tf_op jit(solution)/shard_map/all_to_all | solution.py:92
Sparse Core Ops, SparseCore 0:
  58.6 62.3 all-gather.2
where the time goes:
time: 181 us
  blocking collectives  69.2 us (38%)
  waiting for transfers between devices  31.7 us (18%)
  starting transfers between devices  20.9 us (12%)
  other arithmetic  20.1 us (11%)
  between operations  14.5 us (8%)
  local copies, waits for them, and re-layouts  12.7 us (7%)
  matrix products  11.7 us (6%)
    all_gather x1, blocking collectives, per_device(): lax.all_gather(logs, 'dev', axis=0, tiled=True)  35.5 us
    all_gather x1, blocking collectives, per_device(): lax.all_gather(target, 'dev', axis=0, tiled=True)  33.7 us
    all_to_all x1, waiting for transfers between devices, per_device(): lax.all_to_all(buckets, 'dev', split_axis=1, concat_axis=1, tiled=True)  13.5 us
    all_to_all x1, waiting for transfers between devices, per_device(): lax.all_to_all(slot_grad.reshape(nparam, ndev, cap), 'dev', split_axis=1,...  13 us
    all_to_all x1, starting transfers between devices, per_device(): lax.all_to_all(wanted, 'dev', split_axis=0, concat_axis=0, tiled=True)  11.5 us
    scatter-add x1, other arithmetic, per_device(): slot_grad = jnp.zeros((nparam, ndev * cap), jnp.float32).at[:, seg_ids.re...  6.79 us
    scatter-add x1, other arithmetic, per_device(): grad = jnp.zeros((nparam, owned), jnp.float32).at[:, received.reshape(-1)...  6.18 us
    all_to_all x1, waiting for transfers between devices, per_device(): lax.all_to_all(wanted, 'dev', split_axis=0, concat_axis=0, tiled=True)  5.21 us
  transfers between devices with their start and end apart: 4, of which 3 were waited for; matrix products, arithmetic and copies ran while one was open for 5% of the time, Pallas kernels for 0%

commit v1 on v0

--- a/solution.py
+++ b/solution.py
@@ -61,7 +61,9 @@
     all_colours, all_logs, all_target = (
         lax.all_gather(colours, "dev", axis=0, tiled=True),
         lax.all_gather(logs, "dev", axis=0, tiled=True),
-        lax.all_gather(target, "dev", axis=0, tiled=True),
+        jnp.concatenate(
+            lax.all_to_all(jnp.stack([target] * lax.axis_size("dev")), "dev", 0, 0), axis=0
+        ),
     )
     total = all_logs.shape[0]
     ntiles = all_target.shape[0]

time: 181 us -> 173 us (0.956)
  blocking collectives: 69.2 us -> 38 us
  waiting for transfers between devices: 31.7 us -> 47.8 us
  starting transfers between devices: 20.9 us -> 26.3 us
    all_gather x1 -> x0, blocking collectives: 33.7 us -> none  [per_device(): lax.all_gather(target, 'dev', axis=0, tiled=True)]
    all_gather x1, waiting for transfers between devices: 0.02 us -> 16.1 us  [per_device(): lax.all_gather(colours, 'dev', axis=0, tiled=True)]
    all_to_all x0 -> x1, starting transfers between devices: none -> 4.71 us  [per_device(): lax.all_to_all(jnp.stack([target] * lax.axis_size('dev')), 'dev', 0, 0)]
    all_gather x1, blocking collectives: 35.5 us -> 38 us  [per_device(): lax.all_gather(logs, 'dev', axis=0, tiled=True)]
  transfers between devices with their start and end apart: 4 -> 5, of which waited for: 3 -> 4; matrix products, arithmetic and copies ran while one was open for 5% -> 6% of each run, Pallas kernels for 0% -> 0%
where the time goes in v1:
time: 173 us; the launch traced here: 172 us
  waiting for transfers between devices  47.8 us (28%)
  blocking collectives  38 us (22%)
  starting transfers between devices  26.3 us (15%)
  other arithmetic  20.1 us (12%)
  between operations  14.5 us (8%)
  local copies, waits for them, and re-layouts  14 us (8%)
  matrix products  11.7 us (7%)
    all_gather x1, blocking collectives, per_device(): lax.all_gather(logs, 'dev', axis=0, tiled=True)  38 us
    all_gather x1, waiting for transfers between devices, per_device(): lax.all_gather(colours, 'dev', axis=0, tiled=True)  16.1 us
    all_to_all x1, waiting for transfers between devices, per_device(): lax.all_to_all(buckets, 'dev', split_axis=1, concat_axis=1, tiled=True)  13.5 us
    all_to_all x1, waiting for transfers between devices, per_device(): lax.all_to_all(slot_grad.reshape(nparam, ndev, cap), 'dev', split_axis=1,...  13 us
    all_to_all x1, starting transfers between devices, per_device(): lax.all_to_all(wanted, 'dev', split_axis=0, concat_axis=0, tiled=True)  11.5 us
    scatter-add x1, other arithmetic, per_device(): slot_grad = jnp.zeros((nparam, ndev * cap), jnp.float32).at[:, seg_ids.re...  6.79 us
    scatter-add x1, other arithmetic, per_device(): grad = jnp.zeros((nparam, owned), jnp.float32).at[:, received.reshape(-1)...  6.18 us
    all_to_all x1, starting transfers between devices, per_device(): lax.all_to_all(slot_grad.reshape(nparam, ndev, cap), 'dev', split_axis=1,...  5.32 us
  transfers between devices with their start and end apart: 5, of which 4 were waited for; matrix products, arithmetic and copies ran while one was open for 6% of the time, Pallas kernels for 0%

profile of v1, /device:TPU:1, one launch (start us, length us, event | category | flops | bytes accessed | tf_op | source)
XLA Modules:
  0.0 172.4 jit_solution(5935603426681092728)
XLA Ops:
  7.2 1.4 copy.92
  8.6 11.5 %all-to-all-start = ((s32[128,1,8]{2,1,0:T(1,128)}), s32[128,1,8]{2,1,0:T(1,128)S(1)}, u32[]{:S(2)}, u32[]{:S(2)}) async-start(s32[128,1,8]{2,1,0:T(1,128)} %bitcast), calls=%async_computation | async-start | bytes 131072 | tf_op jit(solution)/shard_map/all_to_all | solution.py:47
  20.1 0.7 fusion.92
  20.8 0.7 compare_and_fusion.1
  21.5 0.8 and_select_fusion
  22.3 0.8 fusion.102
  23.0 0.1 broadcast_add_fusion.1
  23.1 1.1 copy.93
  24.2 5.2 %all-to-all-done = s32[128,1,8]{2,1,0:T(1,128)S(1)} async-done(((s32[128,1,8]{2,1,0:T(1,128)}), s32[128,1,8]{2,1,0:T(1,128)S(1)}, u32[]{:S(2)}, u32[]{:S(2)}) %all-to-all-start) | async-done | bytes 4128 | tf_op jit(solution)/shard_map/all_to_all | solution.py:47
  29.4 0.1 reshape.399
  29.5 2.8 %gather_fusion = f32[1024,9]{1,0:T(8,128)S(1)} fusion(f32[9,1024]{0,1:T(8,128)S(1)} %copy.93, s32[1024]{0:T(1024)S(1)} %broadcast_clamp_fusion.1), kind=kCustom, calls=%fused_computation | custom fusion | bytes 77824 | tf_op jit(solution)/shard_map/jit(_take)/gather | solution.py:48
  32.3 0.0 copy-start.6
  32.4 1.0 fusion.43
  33.4 4.8 %all-to-all-start.1 = ((f32[9,128,8]{0,2,1:T(8,128)}), f32[9,128,8]{0,2,1:T(8,128)S(1)}, u32[]{:S(2)}, u32[]{:S(2)}) async-start(f32[9,128,8]{0,2,1:T(8,128)} %fusion.43), calls=%async_computation.1 | async-start | bytes 1048576 | tf_op jit(solution)/shard_map/all_to_all | solution.py:49
  38.1 0.0 all-gather.3.cloned.1.call-start
  38.2 13.5 %all-to-all-done.1 = f32[9,128,8]{0,2,1:T(8,128)S(1)} async-done(((f32[9,128,8]{0,2,1:T(8,128)}), f32[9,128,8]{0,2,1:T(8,128)S(1)}, u32[]{:S(2)}, u32[]{:S(2)}) %all-to-all-start.1) | async-done | bytes 36896 | tf_op jit(solution)/shard_map/all_to_all | solution.py:49
  51.7 2.8 %gather_fusion.1 = f32[1024,9]{1,0:T(8,128)S(1)} fusion(f32[9,1024]{0,1:T(8,128)S(1)} %bitcast.119, s32[1024]{0:T(1024)S(1)} %broadcast_clamp_fusion), kind=kCustom, calls=%fused_computation.1 | custom fusion | bytes 77824 | tf_op jit(solution)/shard_map/jit(_take)/gather | solution.py:55
  54.5 0.2 copy.95
  54.8 0.1 bitcast_select_fusion.1
  54.9 1.5 convolution_exponential_fusion
  56.3 0.0 copy-start.7
  56.3 0.0 copy-start.5
  56.4 0.0 copy-start.3
  56.4 0.0 copy-start.4
  56.4 2.1 %fusion.60 = f32[4,3,256]{2,1,0:T(4,128)} fusion(f32[256,4,256]{0,2,1:T(8,128)S(1)} %convolution_exponential_fusion, f32[4,256]{1,0:T(4,128)S(1)} %get-tuple-element.52, f32[4,256]{1,0:T(4,128)S(1)} %get-tuple-element.55, f32[4,256]{1,0:T(4,128)S(1)} %get-tuple-element.60, f32[4,256]{1,0:T(4,128)S(1)} %get-tuple-element.48, ...), kind=kOutput, calls=%fused_computation.86 | convolution fusion | flops 12845056 | bytes 1110016 | tf_op jit(solution)/shard_map/jvp(vmap())/dot_general | solution.py:34
  58.5 0.0 copy-done.7
  58.5 0.0 all-gather.3.cloned.1.call-update
  58.5 0.9 stack.2
  59.5 4.7 %all-to-all-start.2 = ((f32[128,1,3,256]{3,1,2,0:T(1,128)}), f32[128,1,3,256]{3,1,2,0:T(1,128)S(1)}, u32[]{:S(2)}, u32[]{:S(2)}) async-start(f32[128,1,3,256]{3,1,2,0:T(1,128)} %stack.2), calls=%async_computation.2 | async-start | bytes 786432 | tf_op jit(solution)/shard_map/all_to_all | solution.py:65
  64.3 0.5 broadcast.502
  64.8 0.8 reduce.3
  65.6 0.1 reshape.387
  65.7 1.0 log-plus-one_reduce_fusion
  66.7 38.0 %all-gather = f32[128,4,256]{2,1,0:T(4,128)S(1)} all-gather(f32[1,4,256]{2,1,0:T(4,128)S(1)} %bitcast.131), channel_id=1, replica_groups=mesh['dev'=128] {'dev'}, dimensions={0}, use_global_device_ids=true | all-gather | bytes 528384 | tf_op jit(solution)/shard_map/all_gather | solution.py:63
  104.7 0.2 reshape.433
  104.9 0.7 convolution_exponential_fusion.1
  105.6 0.2 copy.96
  105.9 0.0 all-to-all-done.2
  105.9 0.6 copy.99
  106.5 0.2 copy.100
  106.6 16.1 %all-gather.3.cloned.1.call-done = f32[512,3,256]{2,1,0:T(4,128)} async-done(((f32[4,3,256]{2,1,0:T(4,128)}), f32[512,3,256]{2,1,0:T(4,128)}) %all-gather.3.cloned.1.call-update) | async-done | bytes 1572880 | tf_op jit(solution)/shard_map/all_gather | solution.py:62
  122.7 1.8 %copy.98 = f32[512,3,256]{0,2,1:T(8,128)S(1)} copy(f32[512,3,256]{2,1,0:T(4,128)} %all-gather.3.cloned.1.call-done) | data formatting | bytes 3145728 | tf_op jit(solution)/shard_map/all_gather | solution.py:62
  124.5 0.2 broadcast_multiply_fusion
  124.8 0.0 copy-start.8
  124.8 1.0 fusion.66
  125.8 0.3 fusion.61
  126.1 1.1 fusion.72
  127.1 1.2 fusion.59
  128.3 0.8 fusion.12
  129.2 3.0 %fusion.33 = (f32[4,256]{1,0:T(4,128)S(1)}, f32[4,256]{1,0:T(4,128)S(1)}, f32[4,256]{1,0:T(4,128)S(1)}, f32[4,256]{1,0:T(4,128)S(1)}, f32[4,256]{1,0:T(4,128)S(1)}, /*index=5*/f32[4,256]{1,0:T(4,128)S(1)}) fusion(f32[4,256]{1,0:T(4,128)S(1)} %get-tuple-element.55, f32[4,256]{1,0:T(4,128)S(1)} %get-tuple-element.60, f32[4,256]{1,0:T(4,128)S(1)} %get-tuple-element.52, ...), kind=kOutput, calls=%fused_computation.52 | convolution fusion | flops 820570112 | bytes 2183168 | tf_op jit(solution)/shard_map/transpose(jvp(vmap()))/dot_general | solution.py:32
  132.3 0.1 fusion.81
  132.4 0.1 add_bitcast_fusion
  132.5 0.2 copy.105
  132.8 0.0 copy-start
  132.8 0.0 copy-start.1
  132.8 0.0 copy-start.2
  132.8 6.8 %scatter_custom_fusion = f32[9,1024]{0,1:T(8,128)} fusion(s32[1024]{0:T(1024)S(1)} %bitcast.134, f32[1024,9]{1,0:T(8,128)S(1)} %copy.105, f32[]{:T(128)} %constant.149.clone.1), kind=kCustom, calls=%fused_computation.90 | custom fusion | flops 9216 | bytes 36868 | tf_op jit(solution)/shard_map/scatter-add | solution.py:92
  139.6 5.3 %all-to-all-start.3 = ((f32[9,128,8]{0,2,1:T(8,128)}), f32[9,128,8]{0,2,1:T(8,128)S(1)}, u32[]{:S(2)}, u32[]{:S(2)}) async-start(f32[9,128,8]{0,2,1:T(8,128)} %bitcast.30), calls=%async_computation.3 | async-start | bytes 1048576 | tf_op jit(solution)/shard_map/all_to_all | solution.py:94
  144.9 0.6 constant_dynamic-slice_fusion.1
  145.5 13.0 %all-to-all-done.3 = f32[9,128,8]{0,2,1:T(8,128)S(1)} async-done(((f32[9,128,8]{0,2,1:T(8,128)}), f32[9,128,8]{0,2,1:T(8,128)S(1)}, u32[]{:S(2)}, u32[]{:S(2)}) %all-to-all-start.3) | async-done | bytes 36896 | tf_op jit(solution)/shard_map/all_to_all | solution.py:94
  158.5 6.2 %scatter_custom_fusion.1 = f32[9,1024]{0,1:T(8,128)S(1)} fusion(s32[1024]{0:T(1024)S(1)} %bitcast.133, f32[9,128,8]{0,2,1:T(8,128)S(1)} %all-to-all-done.3, f32[]{:T(128)} %constant.149.clone.1), kind=kCustom, calls=%fused_computation.67 | custom fusion | flops 9216 | bytes 561156 | tf_op jit(solution)/shard_map/scatter-add | solution.py:100
  164.6 0.2 copy.106
  164.8 0.0 copy-done.2
  164.9 0.7 divide_subtract_fusion
  (36 shorter events, 0.3 us)
Async XLA Ops:
  8.6 20.8 %all-to-all-start = ((s32[128,1,8]{2,1,0:T(1,128)}), s32[128,1,8]{2,1,0:T(1,128)S(1)}, u32[]{:S(2)}, u32[]{:S(2)}) async-start(s32[128,1,8]{2,1,0:T(1,128)} %bitcast), calls=%async_computation | async-start | bytes 131072 | tf_op jit(solution)/shard_map/all_to_all | solution.py:47
  32.3 22.4 %copy-start.6 = (s32[4]{0:T(128)S(1)}, s32[4]{0:T(128)}, u32[]{:S(2)}) copy-start(s32[4]{0:T(128)} %param.13) | copy-start | bytes 52
  33.4 18.3 %all-to-all-start.1 = ((f32[9,128,8]{0,2,1:T(8,128)}), f32[9,128,8]{0,2,1:T(8,128)S(1)}, u32[]{:S(2)}, u32[]{:S(2)}) async-start(f32[9,128,8]{0,2,1:T(8,128)} %fusion.43), calls=%async_computation.1 | async-start | bytes 1048576 | tf_op jit(solution)/shard_map/all_to_all | solution.py:49
  38.1 84.6 %all-gather.3.cloned.1.call-start = ((), (), s32[]{:S(2)}) async-start(), calls=%async_computation.4 | async-start | bytes 2113536 | tf_op jit(solution)/shard_map/all_gather | solution.py:62
  56.3 2.1 %copy-start.7 = (f32[256,4,256]{0,2,1:T(8,128)}, f32[256,4,256]{0,2,1:T(8,128)S(1)}, u32[]{:S(2)}) copy-start(f32[256,4,256]{0,2,1:T(8,128)S(1)} %convolution_exponential_fusion) | copy-start | bytes 3145732
  56.3 2.2 %copy-start.5 = (f32[1,3,256]{2,0,1:T(1,128)S(1)}, f32[1,3,256]{2,0,1:T(1,128)}, u32[]{:S(2)}) copy-start(f32[1,3,256]{2,0,1:T(1,128)} %param.15) | copy-start | bytes 9220
  56.4 7.8 %copy-start.3 = (s32[4,256]{1,0:T(4,128)S(1)}, s32[4,256]{1,0:T(4,128)}, u32[]{:S(2)}) copy-start(s32[4,256]{1,0:T(4,128)} %param.12) | copy-start | bytes 12292
  56.4 7.9 %copy-start.4 = (s32[512]{0:T(512)S(1)}, s32[512]{0:T(512)}, u32[]{:S(2)}) copy-start(s32[512]{0:T(512)} %param.14) | copy-start | bytes 6148
  59.5 46.4 %all-to-all-start.2 = ((f32[128,1,3,256]{3,1,2,0:T(1,128)}), f32[128,1,3,256]{3,1,2,0:T(1,128)S(1)}, u32[]{:S(2)}, u32[]{:S(2)}) async-start(f32[128,1,3,256]{3,1,2,0:T(1,128)} %stack.2), calls=%async_computation.2 | async-start | bytes 786432 | tf_op jit(solution)/shard_map/all_to_all | solution.py:65
  124.8 2.4 %copy-start.8 = (f32[256,4,256]{0,2,1:T(8,128)S(1)}, f32[256,4,256]{0,2,1:T(8,128)}, u32[]{:S(2)}) copy-start(f32[256,4,256]{0,2,1:T(8,128)} %copy-done.7) | copy-start | bytes 3145732
  132.8 32.1 %copy-start = (f32[9,1024]{1,0:T(8,128)S(1)}, f32[9,1024]{1,0:T(8,128)}, u32[]{:S(2)}) copy-start(f32[9,1024]{1,0:T(8,128)} %param.8) | copy-start | bytes 110596
  132.8 32.1 %copy-start.1 = (f32[9,1024]{1,0:T(8,128)S(1)}, f32[9,1024]{1,0:T(8,128)}, u32[]{:S(2)}) copy-start(f32[9,1024]{1,0:T(8,128)} %param.9) | copy-start | bytes 110596
  132.8 32.1 %copy-start.2 = (f32[9,1024]{1,0:T(8,128)S(1)}, f32[9,1024]{1,0:T(8,128)}, u32[]{:S(2)}) copy-start(f32[9,1024]{1,0:T(8,128)} %param.10) | copy-start | bytes 110596
  139.6 18.9 %all-to-all-start.3 = ((f32[9,128,8]{0,2,1:T(8,128)}), f32[9,128,8]{0,2,1:T(8,128)S(1)}, u32[]{:S(2)}, u32[]{:S(2)}) async-start(f32[9,128,8]{0,2,1:T(8,128)} %bitcast.30), calls=%async_computation.3 | async-start | bytes 1048576 | tf_op jit(solution)/shard_map/all_to_all | solution.py:94
Sparse Core Ops, SparseCore 0:
  58.6 64.0 all-gather.2
